TPU v7x, 32 devices: a whole 2x2x4 slice. The times are simulated.
32 devices in a mesh: groups: 2 (over x), gx: 8 (over z, y), gy: 2 (over core).
Axes of the slice: x: 2, y: 2, z: 4, core: 2. Of those that a mesh axis runs over, the one named last changes fastest.
Arguments:
- initial_voltage: float32 [256, 128, 256], P(('groups', 'gx'), 'gy'), parts along dimension 0, may hold values from -0.1 to 1.1
- conductivity: float32 [256, 128, 256], P(('groups', 'gx'), 'gy'), parts along dimension 0, may hold values from 0.3 to 1.2
- tissue_mask: int32 [256, 128, 256], P(('groups', 'gx'), 'gy'), parts along dimension 0, may hold values 0 or 1
- target_step: int32 [256, 128, 256], P(('groups', 'gx'), 'gy'), parts along dimension 0, may hold values from 0 to 8
- initial_purkinje: float32 [16384, 128], P(('groups', 'gx', 'gy')), parts along dimension 0, may hold values from -0.1 to 1.1
- purkinje_conductivity: float32 [16384], P(('groups', 'gx', 'gy')), parts along dimension 0, may hold values from 0.5 to 4
- segment_parent: int32 [16384], P(('groups', 'gx', 'gy')), parts along dimension 0, may hold values from -1 to 8190, as said below
- purkinje_target: int32 [16384, 128], P(('groups', 'gx', 'gy')), parts along dimension 0, may hold values from 0 to 8
- junction_voxel: int32 [16384], P(('groups', 'gx', 'gy')), parts along dimension 0, may hold values from 0 to 4194303, as said below
- junction_node: int32 [16384], P(('groups', 'gx', 'gy')), parts along dimension 0, may hold values from 0 to 1048575, as said below
Outputs:
- final_voltage: float32 [256, 128, 256], P(('groups', 'gx'), 'gy'), parts along dimension 0
- final_purkinje: float32 [16384, 128], P(('groups', 'gx', 'gy')), parts along dimension 0
- conductivity_gradient: float32 [256, 128, 256], P(('groups', 'gx'), 'gy'), parts along dimension 0
- purkinje_gradient: float32 [16384], P(('groups', 'gx', 'gy')), parts along dimension 0
- voltage_adjoint: float32 [256, 128, 256], P(('groups', 'gx'), 'gy'), parts along dimension 0
- purkinje_adjoint: float32 [16384, 128], P(('groups', 'gx', 'gy')), parts along dimension 0
There are 2 independent parts, one for each index of `groups`. A program takes and returns all parts, laid end to end along the dimension named above; each array names one. Nothing has to cross between parts.
Inputs may be any that keep to these rules, and one draw needn't show every extreme that they name: `junction_voxel`: A flat voxel index (x * 128 + y) * 256 + z. Among the 512 entries of one device's block, at most 64 lie in the voxel block of one tissue device, and some tissue device holds exactly 64 junctions of every device's block. `junction_node`: A flat node index s * 128 + i; the segment s of entry k lies in the same device block as entry k (block k // 512). `segment_parent`: -1 marks a root; otherwise the number of an earlier segment, at most 1024 before it.
All inputs are finite; a program needn't handle non-finite values. No bound on the sum of `tissue_mask` on one device may be relied on, other than what follows from the above.
Results may differ from a plain program's by a relative error of at most 0.0001.
Values sent between devices are 32-bit elements; how exact they have to be, the bound alone decides.
A program may use at most 128 MiB of HBM per device.

v0:
```python
import functools

import jax
import jax.numpy as jnp
from jax import lax
from jax.experimental import pallas as pl
from jax.experimental.pallas import tpu as pltpu
from jax.sharding import PartitionSpec as P

time_step = 0.05
gap_conductance = 4.0
ion_rate = 8.0
threshold = 0.15
loss_weight = 10.0
target_span = 8.0
LANES = 128
F32 = jnp.float32
BF16 = jnp.bfloat16


def ionic(values):
    return ion_rate * values * (values - threshold) * (1.0 - values)


def slope(values):
    return ion_rate * (-3.0 * values * values + 2.0 * (1.0 + threshold) * values - threshold)


def pieces(values):
    high = values.astype(BF16)
    return high, (values - high.astype(F32)).astype(BF16)


def dot(a, b):
    return lax.dot_general(a, b, (((1,), (0,)), ((), ())), preferred_element_type=F32)


def kernel(
    grid_x, grid_y, cap,
    v0_h, sigma_h, mask_h, target_h, y0_h, sigma_row, parent_row, ptarget_h, slot_voxel, slot_node,
    v2_o, y2_o, gs_o, gp_o, la_o, mu_o,
    vp, hys, hyr, tmp_mask, target, gxf, gym, gyp, gzm, gzp, v2b, l0b, gsb,
    ys, y2b, mu0b, ptarget, pb, sb, ptb, pgb,
    ot, ott, lm, xs, ws, op, opt, lmp, yss, wps,
    qt, qp, ta, tb, colb, colp, send, recv, voxr,
    tails, heads, tailr, headr, kids, kidr,
    loc_sem, js, jr, vs, vr, xs_s, xs_r, ysm_s, ysm_r, cs_s, cs_r, ks_s, ks_r,
):
    D = grid_x * grid_y
    cx, cy, cz = v2b.shape
    S, N = y2b.shape
    slots = D * cap
    rows = cx * cy
    gx = lax.axis_index("gx")
    gy = lax.axis_index("gy")
    me = gx * grid_y + gy

    def dev(flat):
        return {"gx": lax.div(flat, grid_y), "gy": lax.rem(flat, grid_y)}

    def rc(src, dst, s, r, where):
        return pltpu.make_async_remote_copy(
            src_ref=src, dst_ref=dst, send_sem=s, recv_sem=r,
            device_id=where, device_id_type=pl.DeviceIdType.MESH,
        )

    loads = [
        pltpu.make_async_copy(v0_h, vp.at[0, pl.ds(1, cx)], loc_sem.at[0]),
        pltpu.make_async_copy(sigma_h, gsb, loc_sem.at[1]),
        pltpu.make_async_copy(mask_h, tmp_mask, loc_sem.at[2]),
        pltpu.make_async_copy(y0_h, ys.at[0], loc_sem.at[3]),
        pltpu.make_async_copy(target_h, target, loc_sem.at[4]),
        pltpu.make_async_copy(ptarget_h, ptarget, loc_sem.at[5]),
    ]
    for c in loads:
        c.start()

    barrier = pltpu.get_barrier_semaphore()

    def greet(o, _):
        pl.semaphore_signal(
            barrier, inc=1, device_id=dev(lax.rem(me + o, D)), device_id_type=pl.DeviceIdType.MESH
        )
        return 0

    lax.fori_loop(1, D, greet, 0)
    kids[0:1, :] = sigma_row[...]
    kids[1:2, :] = parent_row[...]
    pl.semaphore_wait(barrier, D - 1)

    def vox_copy(o):
        to = lax.rem(me + o, D)
        return rc(slot_voxel.at[to], voxr.at[me], vs.at[o], vr.at[o], dev(to))

    def junction_copy(k, o):
        to = lax.rem(me + o, D)
        return rc(send.at[k, to], recv.at[k, me], js.at[k, o], jr.at[k, o], dev(to))

    def over_partners(make, act):
        def step(o, _):
            act(make(o))
            return 0

        lax.fori_loop(1, D, step, 0)

    def kid_copy(j):
        return rc(kids, kidr.at[j - 1], ks_s.at[j - 1], ks_r.at[j - 1], dev(lax.rem(me + D - j, D)))

    def cable_copies(k):
        out = []
        for j in (1, 2):
            out.append(rc(tails.at[k], tailr.at[k, j - 1], cs_s.at[k, j - 1], cs_r.at[k, j - 1],
                          dev(lax.rem(me + j, D))))
            out.append(rc(heads.at[k], headr.at[k, j - 1], cs_s.at[k, j + 1], cs_r.at[k, j + 1],
                          dev(lax.rem(me + D - j, D))))
        return out

    def up_copy(k):
        return rc(vp.at[k, cx], vp.at[k, 0], xs_s.at[k, 0], xs_r.at[k, 0],
                  {"gx": lax.rem(gx + 1, grid_x), "gy": gy})

    def down_copy(k):
        return rc(vp.at[k, 1], vp.at[k, cx + 1], xs_s.at[k, 1], xs_r.at[k, 1],
                  {"gx": lax.rem(gx + grid_x - 1, grid_x), "gy": gy})

    def side_copy(k):
        return rc(hys.at[k], hyr.at[k], ysm_s.at[k], ysm_r.at[k], {"gx": gx, "gy": 1 - gy})

    def halo_start(k):
        @pl.when(gx < grid_x - 1)
        def _():
            up_copy(k).start()

        @pl.when(gx > 0)
        def _():
            down_copy(k).start()

        side_copy(k).start()

    def halo_wait(k):
        @pl.when(gx > 0)
        def _():
            up_copy(k).wait_recv()

        @pl.when(gx < grid_x - 1)
        def _():
            down_copy(k).wait_recv()

        side_copy(k).wait_recv()

    def halo_sent(k):
        @pl.when(gx < grid_x - 1)
        def _():
            up_copy(k).wait_send()

        @pl.when(gx > 0)
        def _():
            down_copy(k).wait_send()

        side_copy(k).wait_send()

    over_partners(vox_copy, lambda c: c.start())
    for j in (1, 2):
        kid_copy(j).start()
    voxr[me] = slot_voxel[me]

    zero_plane = jnp.zeros((cy, cz), F32)

    @pl.when(gx == 0)
    def _():
        for k in range(5):
            vp[k, 0] = zero_plane

    @pl.when(gx == grid_x - 1)
    def _():
        for k in range(5):
            vp[k, cx + 1] = zero_plane

    def split_plane(i, c):
        high, low = pieces(c)
        at = pl.ds(pl.multiple_of(i * cy, cy), cy)
        xs[at, 0:cz] = high
        xs[at, cz : 2 * cz] = low

    def edge_row(c):
        return jnp.where(gy == 0, c[cy - 1 : cy, :], c[0:1, :])

    for n in range(4):
        loads[n].wait()

    def prepare(i, _):
        masked = gsb[i] * tmp_mask[i].astype(F32)
        vp[4, i + 1] = masked
        hys[4, pl.ds(i, 1), :] = edge_row(masked)
        c = vp[0, i + 1]
        hys[0, pl.ds(i, 1), :] = edge_row(c)
        split_plane(i, c)
        return 0

    lax.fori_loop(0, cx, prepare, 0)
    halo_start(0)
    halo_start(4)

    def cable_start(k):
        y = ys[k]
        turned = jnp.transpose(y)
        tails[k] = turned[N - 1 : N, :]
        heads[k] = turned[0:1, :]
        for c in cable_copies(k):
            c.start()
        high, low = pieces(y)
        yss[:, 0:N] = high
        yss[:, N : 2 * N] = low

    cable_start(0)
    pb[...] = jnp.transpose(jnp.broadcast_to(parent_row[...], (LANES, S)))
    sb[...] = jnp.transpose(jnp.broadcast_to(sigma_row[...], (LANES, S)))
    pgb[...] = jnp.zeros_like(pgb)

    def build(source, width, depth, onehot, onehot_t, lane_mask, column):
        ta[...] = jnp.zeros_like(ta)
        for d in range(D):
            ta[d : d + 1, :] = source[d]
        index = jnp.transpose(ta[...])[:cap, :]
        row = jnp.floor(index * (1.0 / width))
        lane = index - row * width
        lane_of = lax.broadcasted_iota(jnp.int32, (1, width), 1).astype(F32)
        row_of = lax.broadcasted_iota(jnp.int32, (1, depth), 1).astype(F32)
        for d in range(D):
            at = slice(d * cap, (d + 1) * cap)
            r = row[:, d : d + 1]
            onehot[at, :] = jnp.where(r == row_of, 1.0, 0.0).astype(BF16)
            lane_mask[at, :] = jnp.where(lane[:, d : d + 1] == lane_of, 1.0, 0.0)
            column[at, :] = jnp.broadcast_to(r, (cap, LANES))
        row_line = jnp.transpose(column[...])[0:1, :]
        step = 64

        def fill(b, _):
            ids = (lax.broadcasted_iota(jnp.int32, (step, 1), 0) + b * step).astype(F32)
            onehot_t[pl.ds(pl.multiple_of(b * step, step), step), :] = jnp.where(
                ids == row_line, 1.0, 0.0
            ).astype(BF16)
            return 0

        lax.fori_loop(0, depth // step, fill, 0)

    build(slot_node, N, S, op, opt, lmp, colp)
    over_partners(vox_copy, lambda c: c.wait_recv())
    build(voxr, cz, rows, ot, ott, lm, colb)

    lane_id = lax.broadcasted_iota(jnp.int32, (1, LANES), 1)
    block = min(slots, 512)
    per_block = block // cap
    qt[...] = jnp.zeros_like(qt)
    qp[...] = jnp.zeros_like(qp)

    def gather(k):
        def step(b, carry):
            tissue, cable = carry
            at = pl.ds(pl.multiple_of(b * block, block), block)
            got = dot(ot[at, :], xs[...])
            got = (got[:, :cz] + got[:, cz:]) * lm[at, :]
            line = jnp.sum(got, axis=1, keepdims=True)
            gop = dot(op[at, :], yss[...])
            gop = (gop[:, :N] + gop[:, N:]) * lmp[at, :]
            linp = jnp.sum(gop, axis=1, keepdims=True)
            for j in range(per_block):
                here = lane_id == b * per_block + j
                tissue = jnp.where(here, line[j * cap : (j + 1) * cap], tissue)
                cable = jnp.where(here, linp[j * cap : (j + 1) * cap], cable)
            return tissue, cable

        zero = jnp.zeros((cap, LANES), F32)
        tissue, cable = lax.fori_loop(0, slots // block, step, (zero, zero))
        qt[0:cap, :] = tissue
        qp[0:cap, :] = cable
        turned_t = jnp.transpose(qt[...])
        turned_p = jnp.transpose(qp[...])
        for d in range(D):
            send[k, d, 0:1, :] = turned_p[d : d + 1, :]
            send[k, d, 1:2, :] = turned_t[d : d + 1, :]
        over_partners(functools.partial(junction_copy, k), lambda c: c.start())
        recv[k, me] = send[k, me]

    def currents(k):
        over_partners(functools.partial(junction_copy, k), lambda c: c.wait_recv())
        for d in range(D):
            ta[d : d + 1, :] = recv[k, d, 0:1, :]
            tb[d : d + 1, :] = recv[k, d, 1:2, :]
        rate = time_step * gap_conductance
        into_t = rate * (jnp.transpose(ta[...])[:cap, :] - qt[0:cap, :])
        into_p = rate * (qp[0:cap, :] - jnp.transpose(tb[...])[:cap, :])
        for d in range(D):
            at = slice(d * cap, (d + 1) * cap)
            high, low = pieces(into_t[:, d : d + 1] * lm[at, :])
            ws[at, 0:cz] = high
            ws[at, cz : 2 * cz] = low
            high, low = pieces(into_p[:, d : d + 1] * lmp[at, :])
            wps[at, 0:N] = high
            wps[at, N : 2 * N] = low

    row_id = lax.broadcasted_iota(jnp.int32, (cy, 1), 0)
    z_id = lax.broadcasted_iota(jnp.int32, (1, cz), 1)

    def beside(k, i):
        c = vp[k, i + 1]
        side = hyr[k, pl.ds(i, 1), :]
        yp = jnp.where(row_id == cy - 1, side, pltpu.roll(c, cy - 1, 0))
        ym = jnp.where(row_id == 0, side, pltpu.roll(c, 1, 0))
        return c, (vp[k, i + 2], vp[k, i], yp, ym, pltpu.roll(c, cz - 1, 1), pltpu.roll(c, 1, 1))

    def weights(i):
        return (gxf[i + 1], gxf[i], gyp[i], gym[i], gzp[i], gzm[i])

    def face(a, b):
        return jnp.where(jnp.minimum(a, b) > 0.0, 0.5 * (a + b), 0.0)

    def faces(i, _):
        c = vp[4, i + 1]
        side = hyr[4, pl.ds(i, 1), :]
        below = jnp.where(gy > 0, side, 0.0)
        above = jnp.where(gy < grid_y - 1, side, 0.0)
        gxf[i] = face(vp[4, i], c)
        gyp[i] = face(c, jnp.where(row_id == cy - 1, above, pltpu.roll(c, cy - 1, 0)))
        gym[i] = face(c, jnp.where(row_id == 0, below, pltpu.roll(c, 1, 0)))
        gzp[i] = face(c, jnp.where(z_id == cz - 1, 0.0, pltpu.roll(c, cz - 1, 1)))
        gzm[i] = face(c, jnp.where(z_id == 0, 0.0, pltpu.roll(c, 1, 1)))
        return 0

    def cable(k, old, out):
        for c in cable_copies(k):
            c.wait_recv()
        if k == 0:
            for j in (1, 2):
                kid_copy(j).wait_recv()
        tail_rows = [tailr[k, 1], tailr[k, 0], tails[k]]
        head_rows = [heads[k], headr[k, 0], headr[k, 1]]
        kid_rows = [kids[...], kidr[0], kidr[1]]
        step = 64

        def part(b, _):
            at = pl.ds(pl.multiple_of(b * step, step), step)
            y = ys[k, at, :]
            p = pb[at, :]
            has = p[:, 0:1] >= 0.0
            p = jnp.where(p >= 0.0, p, -1e6)
            s = sb[at, :]
            tail = y[:, N - 1 : N]
            ids = (lax.broadcasted_iota(jnp.int32, (step, 1), 0) + b * step + me * S).astype(F32)
            up = jnp.zeros((step, LANES), F32)
            down = jnp.zeros((step, LANES), F32)
            for w in range(3):
                for c in range(S // LANES):
                    cut = slice(c * LANES, (c + 1) * LANES)
                    window = (lane_id + ((me + (w - 2)) * S + c * LANES)).astype(F32)
                    up = up + jnp.where(p == window, tail_rows[w][:, cut], 0.0)
                    sk = kid_rows[w][0:1, cut]
                    down = down + jnp.where(
                        kid_rows[w][1:2, cut] == ids, sk * (head_rows[w][:, cut] - tail), 0.0
                    )
            parent_tail = jnp.sum(up, axis=1, keepdims=True)
            inflow = jnp.sum(down, axis=1, keepdims=True)
            head = jnp.where(has, s[:, 0:1] * (parent_tail - y[:, 0:1]), 0.0)
            node = lax.broadcasted_iota(jnp.int32, (1, N), 1)
            step_up = jnp.where(node < N - 1, pltpu.roll(y, N - 1, 1) - y, 0.0)
            edge = s * step_up
            flux = edge - pltpu.roll(edge, 1, 1)
            flux = flux + jnp.where(node == 0, head, 0.0) + jnp.where(node == N - 1, inflow, 0.0)
            if old is None:
                ptb[k, at, :] = jnp.broadcast_to(parent_tail, (step, LANES))
                out[at, :] = y + time_step * (flux + ionic(y))
            else:
                u = ys[old, at, :]
                rise = jnp.where(node < N - 1, pltpu.roll(u, N - 1, 1) - u, 0.0)
                inner = jnp.sum(-step_up * rise, axis=1, keepdims=True)
                over = jnp.where(
                    has, (y[:, 0:1] - parent_tail) * (ptb[old, at, 0:1] - u[:, 0:1]), 0.0
                )
                pgb[at, :] = pgb[at, :] + time_step * (inner + over)
                out[at, :] = y + time_step * (flux + slope(u) * y)
            return 0

        lax.fori_loop(0, S // step, part, 0)

    group = 4 if cx % 4 == 0 else 1

    def spread(finish):
        def step(b, _):
            at = pl.ds(pl.multiple_of(b * (group * cy), group * cy), group * cy)
            add = dot(ott[at, :], ws[...])
            add = add[:, :cz] + add[:, cz:]
            for g in range(group):
                finish(b * group + g, add[g * cy : (g + 1) * cy])
            return 0

        lax.fori_loop(0, cx // group, step, 0)

    def spread_cable():
        add = dot(opt[...], wps[...])
        return add[:, :N] + add[:, N:]

    for k in range(2):
        gather(k)
        if k == 0:
            halo_wait(4)
            lax.fori_loop(0, cx, faces, 0)
            gxf[cx] = face(vp[4, cx], vp[4, cx + 1])
        halo_wait(k)

        def forward(i, _, k=k):
            c, others = beside(k, i)
            total = zero_plane
            for g, n in zip(weights(i), others):
                total = total + g * (n - c)
            new = c + time_step * (total + ionic(c))
            if k == 0:
                vp[1, i + 1] = new
            else:
                v2b[i] = new
            return 0

        lax.fori_loop(0, cx, forward, 0)
        out = ys.at[1] if k == 0 else y2b
        cable(k, None, out)
        currents(k)
        out[...] = out[...] - spread_cable()
        if k == 0:
            def finish(i, add):
                new = vp[1, i + 1] + add
                vp[1, i + 1] = new
                hys[1, pl.ds(i, 1), :] = edge_row(new)
                split_plane(i, new)
        else:
            loads[4].wait()
            loads[5].wait()
            ys[2] = loss_weight * (y2b[...] - (1.0 - ptarget[...].astype(F32) / target_span))

            def finish(i, add):
                new = v2b[i] + add
                v2b[i] = new
                goal = 1.0 - target[i].astype(F32) / target_span
                seed = jnp.where(vp[4, i + 1] > 0.0, loss_weight * (new - goal), 0.0)
                vp[2, i + 1] = seed
                hys[2, pl.ds(i, 1), :] = edge_row(seed)
                split_plane(i, seed)
        cable_start(k + 1)
        spread(finish)
        halo_start(k + 1)

    stores = [
        pltpu.make_async_copy(v2b, v2_o, loc_sem.at[6]),
        pltpu.make_async_copy(y2b, y2_o, loc_sem.at[7]),
    ]
    for c in stores:
        c.start()

    for k in (2, 3):
        old = 3 - k
        gather(k)
        halo_wait(k)

        def backward(i, _, k=k, old=old):
            c, others = beside(k, i)
            v, befores = beside(old, i)
            total = zero_plane
            grad = zero_plane
            for g, n, b in zip(weights(i), others, befores):
                d = n - c
                total = total + g * d
                grad = grad + jnp.where(g > 0.0, d * (v - b), 0.0)
            new = c + time_step * (total + slope(v) * c)
            grad = (0.5 * time_step) * grad
            if k == 2:
                vp[3, i + 1] = new
                gsb[i] = grad
            else:
                l0b[i] = new
                gsb[i] = gsb[i] + grad
            return 0

        lax.fori_loop(0, cx, backward, 0)
        out = ys.at[3] if k == 2 else mu0b
        cable(k, old, out)
        currents(k)
        out[...] = out[...] - spread_cable()
        if k == 2:
            cable_start(3)

            def finish(i, add):
                new = vp[3, i + 1] + add
                vp[3, i + 1] = new
                hys[3, pl.ds(i, 1), :] = edge_row(new)
                split_plane(i, new)
        else:
            stores.append(pltpu.make_async_copy(gsb, gs_o, loc_sem.at[8]))
            stores[-1].start()
            stores.append(pltpu.make_async_copy(mu0b, mu_o, loc_sem.at[9]))
            stores[-1].start()
            gp_o[...] = jnp.transpose(pgb[...])[0:1, :]

            def finish(i, add):
                l0b[i] = l0b[i] + add
        spread(finish)
        if k == 2:
            halo_start(3)

    stores.append(pltpu.make_async_copy(l0b, la_o, loc_sem.at[10]))
    stores[-1].start()
    over_partners(vox_copy, lambda c: c.wait_send())
    for j in (1, 2):
        kid_copy(j).wait_send()
    for k in range(5):
        halo_sent(k)
    for k in range(4):
        over_partners(functools.partial(junction_copy, k), lambda c: c.wait_send())
        for c in cable_copies(k):
            c.wait_send()
    for c in stores:
        c.wait()


def body(
    initial_voltage, conductivity, tissue_mask, target_step, initial_purkinje,
    purkinje_conductivity, segment_parent, purkinje_target, junction_voxel, junction_node,
):
    cx, cy, cz = initial_voltage.shape
    S, N = initial_purkinje.shape
    grid_x = lax.axis_size("gx")
    grid_y = lax.axis_size("gy")
    assert grid_y == 2 and N == LANES
    D = grid_x * grid_y
    per_device = junction_voxel.shape[0]
    cap = max(16, 2 * per_device // D)
    assert cap <= LANES and D <= LANES
    slots = D * cap
    rows = cx * cy

    plane = cy * grid_y * cz
    first = junction_voxel // plane
    rest = junction_voxel % plane
    second = rest // cz
    third = rest % cz
    owner = first // cx * grid_y + second // cy
    local_voxel = (first % cx * cy + second % cy) * cz + third
    local_node = junction_node % (S * N)
    ordinal = jnp.arange(per_device, dtype=jnp.int32)
    same = owner[:, None] == owner[None, :]
    earlier = ordinal[:, None] < ordinal[None, :]
    rank = jnp.sum((same & earlier).astype(jnp.int32), axis=0)
    slot = owner * LANES + rank
    match = jnp.arange(D * LANES, dtype=jnp.int32)[:, None] == slot[None, :]
    slot_voxel = jnp.sum(jnp.where(match, local_voxel[None, :] + 1, 0), axis=1) - 1
    slot_node = jnp.sum(jnp.where(match, local_node[None, :] + 1, 0), axis=1) - 1
    slot_voxel = slot_voxel.astype(F32).reshape(D, 1, LANES)
    slot_node = slot_node.astype(F32).reshape(D, 1, LANES)

    any_spec = pl.BlockSpec(memory_space=pl.ANY)
    vmem = pl.BlockSpec(memory_space=pltpu.VMEM)
    V = pltpu.VMEM
    dma = pltpu.SemaphoreType.DMA
    field = V((cx, cy, cz), F32)
    fibre = V((S, N), F32)
    scratch = [
        V((5, cx + 2, cy, cz), F32), V((5, cx, cz), F32), V((5, cx, cz), F32),
        V((cx, cy, cz), jnp.int32), V((cx, cy, cz), jnp.int32), V((cx + 1, cy, cz), F32),
        field, field, field, field, field, field, field,
        V((4, S, N), F32), fibre, fibre, V((S, N), jnp.int32), V((S, LANES), F32),
        V((S, LANES), F32), V((2, S, LANES), F32), V((S, LANES), F32),
        V((slots, rows), BF16), V((rows, slots), BF16), V((slots, cz), F32),
        V((rows, 2 * cz), BF16), V((slots, 2 * cz), BF16),
        V((slots, S), BF16), V((S, slots), BF16), V((slots, N), F32),
        V((S, 2 * N), BF16), V((slots, 2 * N), BF16),
        V((LANES, LANES), F32), V((LANES, LANES), F32), V((LANES, LANES), F32),
        V((LANES, LANES), F32), V((slots, LANES), F32), V((slots, LANES), F32),
        V((4, D, 2, LANES), F32), V((4, D, 2, LANES), F32), V((D, 1, LANES), F32),
        V((4, 1, S), F32), V((4, 1, S), F32), V((4, 2, 1, S), F32), V((4, 2, 1, S), F32),
        V((2, S), F32), V((2, 2, S), F32),
        dma((11,)), dma((4, D)), dma((4, D)), dma((D,)), dma((D,)),
        dma((5, 2)), dma((5, 2)), dma((5,)), dma((5,)), dma((4, 4)), dma((4, 4)),
        dma((2,)), dma((2,)),
    ]
    tissue = jax.ShapeDtypeStruct((cx, cy, cz), F32)
    cable = jax.ShapeDtypeStruct((S, N), F32)
    v2, y2, gs, gp, la, mu = pl.pallas_call(
        functools.partial(kernel, grid_x, grid_y, cap),
        name="monodomain",
        out_shape=(tissue, cable, tissue, jax.ShapeDtypeStruct((1, S), F32), tissue, cable),
        in_specs=[any_spec] * 5 + [vmem] * 2 + [any_spec] + [vmem] * 2,
        out_specs=(any_spec, any_spec, any_spec, vmem, any_spec, any_spec),
        scratch_shapes=scratch,
        compiler_params=pltpu.CompilerParams(
            collective_id=0, has_side_effects=True, vmem_limit_bytes=62 * 1024 * 1024
        ),
    )(
        initial_voltage, conductivity, tissue_mask, target_step, initial_purkinje,
        purkinje_conductivity.reshape(1, S), segment_parent.astype(F32).reshape(1, S),
        purkinje_target, slot_voxel, slot_node,
    )
    return v2, y2, gs, gp.reshape(S), la, mu


def solution(mesh):
    tissue = P(("groups", "gx"), "gy", None)
    cable = P(("groups", "gx", "gy"), None)
    line = P(("groups", "gx", "gy"))
    return jax.shard_map(
        body,
        mesh=mesh,
        in_specs=(tissue, tissue, tissue, tissue, cable, line, line, cable, line, line),
        out_specs=(tissue, cable, tissue, line, tissue, cable),
        check_vma=False,
    )
```

profile of v0, /device:TPU:0, one launch (start us, length us, event | category | flops | bytes accessed | tf_op | source)
XLA Modules:
  0.0 73.4 jit_solution(9756269082934066173)
XLA Ops:
  0.6 1.3 %convert_element_type.32 = f32[512]{0:T(512)} convert(s32[512]{0:T(512)} %param.16) | non-fusion elementwise | flops 512 | bytes 4096 | tf_op jit(solution)/shard_map/convert_element_type | solution.py:596
  1.9 0.7 fusion.9
  2.6 0.7 fusion.7
  3.3 0.2 convert_reduce_fusion
  3.5 1.2 %select_reduce_fusion = (s32[2048]{0:T(1024)S(1)}, s32[2048]{0:T(1024)S(1)}) fusion(s32[512]{0:T(512)S(1)} %fusion.9, s32[512]{0:T(512)S(1)} %multiply_add_fusion, s32[512]{0:T(512)S(1)} %get-tuple-element.20), kind=kLoop, calls=%fused_computation | loop fusion | flops 5238784 | bytes 22528 | tf_op jit(solution)/shard_map/reduce_sum | solution.py:553
  4.7 0.6 add_convert_fusion
  5.3 61.6 %monodomain.1 = (f32[16,64,256]{2,1,0:T(8,128)}, f32[512,128]{1,0:T(8,128)}, f32[16,64,256]{2,1,0:T(8,128)}, f32[1,512]{1,0:T(1,128)}, f32[16,64,256]{2,1,0:T(8,128)}, /*index=5*/f32[512,128]{1,0:T(8,128)}) custom-call(f32[16,64,256]{2,1,0:T(8,128)} %v0_h.1, f32[16,64,256]{2,1,0:T(8,128)} %sigma_h.1, s32[16,64,256]{2,1,0:T(8,128)} %mask_h.1, ...), custom_call_target="tpu_custom_call" | custom-call | tf_op jit(solution)/shard_map/monodomain/pallas_call | solution.py:584
  66.9 0.0 copy-start.3
  66.9 0.0 copy-start.1
  66.9 2.4 %copy.22 = f32[16,64,256]{2,1,0:T(8,128)} copy(f32[16,64,256]{2,1,0:T(8,128)} %get-tuple-element.30) | data formatting | bytes 2097152
  69.3 0.0 copy-done.3
  69.3 0.7 copy.23
  70.0 0.0 copy-done.1
  70.0 0.0 copy-start.4
  70.0 0.0 copy-start
  70.0 1.0 %copy.24 = f32[16,64,256]{2,1,0:T(8,128)} copy(f32[16,64,256]{2,1,0:T(8,128)S(1)} %copy-done.1) | data formatting | bytes 2097152
  71.0 0.0 copy-done.4
  71.0 0.6 copy.25
  71.6 0.1 copy-done
  71.6 0.0 copy-start.2
  71.6 1.0 %copy.26 = f32[16,64,256]{2,1,0:T(8,128)} copy(f32[16,64,256]{2,1,0:T(8,128)S(1)} %copy-done) | data formatting | bytes 2097152
  72.6 0.1 copy-done.2
  72.7 0.7 copy.27
  (1 shorter events, 0.0 us)
Async XLA Ops:
  66.9 2.4 %copy-start.3 = (f32[512,128]{1,0:T(8,128)S(1)}, f32[512,128]{1,0:T(8,128)}, u32[]{:S(2)}) copy-start(f32[512,128]{1,0:T(8,128)} %get-tuple-element.31) | copy-start | bytes 786436
  66.9 3.1 %copy-start.1 = (f32[16,64,256]{2,1,0:T(8,128)S(1)}, f32[16,64,256]{2,1,0:T(8,128)}, u32[]{:S(2)}) copy-start(f32[16,64,256]{2,1,0:T(8,128)} %get-tuple-element.32) | copy-start | bytes 3145732
  70.0 1.0 %copy-start.4 = (f32[1,512]{1,0:T(1,128)S(1)}, f32[1,512]{1,0:T(1,128)}, u32[]{:S(2)}) copy-start(f32[1,512]{1,0:T(1,128)} %get-tuple-element.15) | copy-start | bytes 6148
  70.0 1.6 %copy-start = (f32[16,64,256]{2,1,0:T(8,128)S(1)}, f32[16,64,256]{2,1,0:T(8,128)}, u32[]{:S(2)}) copy-start(f32[16,64,256]{2,1,0:T(8,128)} %get-tuple-element.34) | copy-start | bytes 3145732
  71.6 1.1 %copy-start.2 = (f32[512,128]{1,0:T(8,128)S(1)}, f32[512,128]{1,0:T(8,128)}, u32[]{:S(2)}) copy-start(f32[512,128]{1,0:T(8,128)} %get-tuple-element.35) | copy-start | bytes 786436
where the time goes:
time: 73.7 us; the launch traced here: 73.4 us
  Pallas kernels  61.6 us (84%)
  local copies, waits for them, and re-layouts  6.5 us (9%)
  other arithmetic  4.66 us (6%)
    pallas_call x1, Pallas kernels, body(): pl.pallas_call(functools.partial(kernel, grid_x, grid_y, cap), name='mono...  61.6 us
    unnamed x16, local copies, waits for them, and re-layouts  6.5 us

commit v1 on v0

--- a/solution.py
+++ b/solution.py
@@ -35,13 +35,34 @@
     return lax.dot_general(a, b, (((1,), (0,)), ((), ())), preferred_element_type=F32)
 
 
+def dot_t(a, b):
+    return lax.dot_general(a, b, (((1,), (1,)), ((), ())), preferred_element_type=F32)
+
+
+def stacked_pieces(values):
+    high = values.astype(BF16)
+    rest = values - high.astype(F32)
+    middle = rest.astype(BF16)
+    return jnp.concatenate([high, middle, (rest - middle.astype(F32)).astype(BF16)], axis=0)
+
+
+def summed(values):
+    n = values.shape[0] // 3
+    return values[:n] + values[n : 2 * n] + values[2 * n :]
+
+
+def bits(size):
+    assert size & (size - 1) == 0
+    return size.bit_length() - 1
+
+
 def kernel(
     grid_x, grid_y, cap,
-    v0_h, sigma_h, mask_h, target_h, y0_h, sigma_row, parent_row, ptarget_h, slot_voxel, slot_node,
+    v0_h, sigma_h, mask_h, target_h, y0_h, sigma_row, parent_int, ptarget_h, junction_voxel, junction_node,
     v2_o, y2_o, gs_o, gp_o, la_o, mu_o,
     vp, hys, hyr, tmp_mask, target, gxf, gym, gyp, gzm, gzp, v2b, l0b, gsb,
-    ys, y2b, mu0b, ptarget, pb, sb, ptb, pgb,
-    ot, ott, lm, xs, ws, op, opt, lmp, yss, wps,
+    ys, y2b, mu0b, ptarget, sb, ends, pgb, pgr, ptr, plt_s, phm, kb, khm, kid_sigma, kid_total,
+    ot, ott, lm, lmb, xs, ws, op, opt, lmp, lmpb, yss, wps, slot_voxel,
     qt, qp, ta, tb, colb, colp, send, recv, voxr,
     tails, heads, tailr, headr, kids, kidr,
     loc_sem, js, jr, vs, vr, xs_s, xs_r, ysm_s, ysm_r, cs_s, cs_r, ks_s, ks_r,
@@ -85,7 +106,41 @@
 
     lax.fori_loop(1, D, greet, 0)
     kids[0:1, :] = sigma_row[...]
-    kids[1:2, :] = parent_row[...]
+    parent_row = parent_int[...].astype(F32)
+    kids[1:2, :] = parent_row
+
+    J = junction_voxel.shape[1]
+    voxel = junction_voxel[...]
+    y_full = cy * grid_y
+    z_at = voxel & (cz - 1)
+    y_at = lax.shift_right_logical(voxel, bits(cz)) & (y_full - 1)
+    x_at = lax.shift_right_logical(voxel, bits(cz) + bits(y_full))
+    owner = lax.shift_right_logical(x_at, bits(cx)) * grid_y + lax.shift_right_logical(y_at, bits(cy))
+    local_voxel = ((x_at & (cx - 1)) * cy + (y_at & (cy - 1))) * cz + z_at
+    local_node = junction_node[...] & (S * N - 1)
+    mine = jnp.where(lax.broadcasted_iota(jnp.int32, (D, J), 0) == owner, 1.0, 0.0)
+    ahead = jnp.where(
+        lax.broadcasted_iota(jnp.int32, (J, J), 0) < lax.broadcasted_iota(jnp.int32, (J, J), 1), 1.0, 0.0
+    ).astype(BF16)
+    rank = jnp.sum(mine * dot(mine.astype(BF16), ahead), axis=0, keepdims=True)
+    rank_t = jnp.where(
+        lax.broadcasted_iota(jnp.int32, (LANES, J), 0).astype(F32) == rank, 1.0, 0.0
+    ).astype(BF16)
+    parts = [mine]
+    for value in (local_voxel, local_node):
+        for shift in (0, 8, 16):
+            digit = (lax.shift_right_logical(value, shift) & 255).astype(F32)
+            parts.append(mine * digit)
+    table = dot_t(jnp.concatenate(parts, axis=0).astype(BF16), rank_t)
+
+    def number(first):
+        a, b, c = (table[(first + n) * D : (first + n + 1) * D] for n in range(3))
+        return a + 256.0 * b + 65536.0 * c + table[:D] - 1.0
+
+    slot_number = number(1)
+    slot_node = number(4)
+    for d in range(D):
+        slot_voxel[d] = slot_number[d : d + 1, :]
     pl.semaphore_wait(barrier, D - 1)
 
     def vox_copy(o):
@@ -213,14 +268,20 @@
         yss[:, N : 2 * N] = low
 
     cable_start(0)
-    pb[...] = jnp.transpose(jnp.broadcast_to(parent_row[...], (LANES, S)))
+    chunks = S // LANES
+    whose = lax.broadcasted_iota(jnp.int32, (LANES, 1), 0).astype(F32)
+    has_parent = parent_row >= 0.0
+    window = jnp.where(has_parent, parent_row - ((me - 2) * S).astype(F32), -1.0)
+    window_high = jnp.floor(window * (1.0 / LANES))
+    plt_s[...] = jnp.where(whose == window - window_high * LANES, 1.0, 0.0).astype(BF16)
+    phm[...] = jnp.where(
+        lax.broadcasted_iota(jnp.int32, phm.shape, 0).astype(F32) == window_high, 1.0, 0.0
+    )
     sb[...] = jnp.transpose(jnp.broadcast_to(sigma_row[...], (LANES, S)))
     pgb[...] = jnp.zeros_like(pgb)
-
-    def build(source, width, depth, onehot, onehot_t, lane_mask, column):
-        ta[...] = jnp.zeros_like(ta)
-        for d in range(D):
-            ta[d : d + 1, :] = source[d]
+    pgr[...] = jnp.zeros_like(pgr)
+
+    def build(width, depth, onehot, onehot_t, lane_mask, lane_mask_b, column):
         index = jnp.transpose(ta[...])[:cap, :]
         row = jnp.floor(index * (1.0 / width))
         lane = index - row * width
@@ -230,7 +291,9 @@
             at = slice(d * cap, (d + 1) * cap)
             r = row[:, d : d + 1]
             onehot[at, :] = jnp.where(r == row_of, 1.0, 0.0).astype(BF16)
-            lane_mask[at, :] = jnp.where(lane[:, d : d + 1] == lane_of, 1.0, 0.0)
+            hit = jnp.where(lane[:, d : d + 1] == lane_of, 1.0, 0.0)
+            lane_mask[at, :] = hit
+            lane_mask_b[at, :] = hit.astype(BF16)
             column[at, :] = jnp.broadcast_to(r, (cap, LANES))
         row_line = jnp.transpose(column[...])[0:1, :]
         step = 64
@@ -244,9 +307,27 @@
 
         lax.fori_loop(0, depth // step, fill, 0)
 
-    build(slot_node, N, S, op, opt, lmp, colp)
+    ta[...] = jnp.zeros_like(ta)
+    ta[0:D, :] = slot_node
+    build(N, S, op, opt, lmp, lmpb, colp)
+    for j in (1, 2):
+        kid_copy(j).wait_recv()
+    kid_rows = [kids[...], kidr[0], kidr[1]]
+    for w in range(3):
+        cut = slice(w * S, (w + 1) * S)
+        near = kid_rows[w][1:2, :] - (me * S).astype(F32)
+        near_high = jnp.floor(near * (1.0 / LANES))
+        hit = jnp.where(whose == near - near_high * LANES, 1.0, 0.0)
+        kb[cut, :] = jnp.transpose(hit).astype(BF16)
+        ids = lax.broadcasted_iota(jnp.int32, (khm.shape[0], 1), 0)
+        ids = jnp.where(ids < chunks, ids, -1000000).astype(F32)
+        khm[:, cut] = jnp.where(ids == near_high, 1.0, 0.0)
+        kid_sigma[:, cut] = kid_rows[w][0:1, :]
+    kid_total[...] = summed(dot(stacked_pieces(khm[...] * kid_sigma[...]), kb[...]))
     over_partners(vox_copy, lambda c: c.wait_recv())
-    build(voxr, cz, rows, ot, ott, lm, colb)
+    for d in range(D):
+        ta[d : d + 1, :] = voxr[d]
+    build(cz, rows, ot, ott, lm, lmb, colb)
 
     lane_id = lax.broadcasted_iota(jnp.int32, (1, LANES), 1)
     block = min(slots, 512)
@@ -290,14 +371,14 @@
         rate = time_step * gap_conductance
         into_t = rate * (jnp.transpose(ta[...])[:cap, :] - qt[0:cap, :])
         into_p = rate * (qp[0:cap, :] - jnp.transpose(tb[...])[:cap, :])
+        high_t, low_t = pieces(into_t)
+        high_p, low_p = pieces(into_p)
         for d in range(D):
             at = slice(d * cap, (d + 1) * cap)
-            high, low = pieces(into_t[:, d : d + 1] * lm[at, :])
-            ws[at, 0:cz] = high
-            ws[at, cz : 2 * cz] = low
-            high, low = pieces(into_p[:, d : d + 1] * lmp[at, :])
-            wps[at, 0:N] = high
-            wps[at, N : 2 * N] = low
+            ws[at, 0:cz] = high_t[:, d : d + 1] * lmb[at, :]
+            ws[at, cz : 2 * cz] = low_t[:, d : d + 1] * lmb[at, :]
+            wps[at, 0:N] = high_p[:, d : d + 1] * lmpb[at, :]
+            wps[at, N : 2 * N] = low_p[:, d : d + 1] * lmpb[at, :]
 
     row_id = lax.broadcasted_iota(jnp.int32, (cy, 1), 0)
     z_id = lax.broadcasted_iota(jnp.int32, (1, cz), 1)
@@ -330,53 +411,48 @@
     def cable(k, old, out):
         for c in cable_copies(k):
             c.wait_recv()
-        if k == 0:
-            for j in (1, 2):
-                kid_copy(j).wait_recv()
         tail_rows = [tailr[k, 1], tailr[k, 0], tails[k]]
-        head_rows = [heads[k], headr[k, 0], headr[k, 1]]
-        kid_rows = [kids[...], kidr[0], kidr[1]]
+        own_heads = heads[k]
+        lines = [t[:, c * LANES : (c + 1) * LANES] for t in tail_rows for c in range(chunks)]
+        pad = phm.shape[0] - len(lines)
+        if pad:
+            lines.append(jnp.zeros((pad, LANES), F32))
+        found = summed(dot(stacked_pieces(jnp.concatenate(lines, axis=0)), plt_s[...]))
+        parent_tail = jnp.sum(phm[...] * found, axis=0, keepdims=True)
+        kid_heads = jnp.concatenate([own_heads, headr[k, 0], headr[k, 1]], axis=1)
+        sums = summed(dot(stacked_pieces(khm[...] * (kid_sigma[...] * kid_heads)), kb[...]))
+        inflow = jnp.concatenate(
+            [
+                sums[c : c + 1] - lines[2 * chunks + c] * kid_total[c : c + 1, :]
+                for c in range(chunks)
+            ],
+            axis=1,
+        )
+        head = jnp.where(has_parent, sigma_row[...] * (parent_tail - own_heads), 0.0)
+        place = lax.broadcasted_iota(jnp.int32, (N, 1), 0)
+        ends[...] = jnp.transpose(
+            jnp.where(place == 0, head, 0.0) + jnp.where(place == N - 1, inflow, 0.0)
+        )
+        if old is None:
+            ptr[k] = parent_tail
+        else:
+            over = (own_heads - parent_tail) * (ptr[old] - heads[old])
+            pgr[...] = pgr[...] + time_step * jnp.where(has_parent, over, 0.0)
         step = 64
+        node = lax.broadcasted_iota(jnp.int32, (1, N), 1)
 
         def part(b, _):
             at = pl.ds(pl.multiple_of(b * step, step), step)
             y = ys[k, at, :]
-            p = pb[at, :]
-            has = p[:, 0:1] >= 0.0
-            p = jnp.where(p >= 0.0, p, -1e6)
-            s = sb[at, :]
-            tail = y[:, N - 1 : N]
-            ids = (lax.broadcasted_iota(jnp.int32, (step, 1), 0) + b * step + me * S).astype(F32)
-            up = jnp.zeros((step, LANES), F32)
-            down = jnp.zeros((step, LANES), F32)
-            for w in range(3):
-                for c in range(S // LANES):
-                    cut = slice(c * LANES, (c + 1) * LANES)
-                    window = (lane_id + ((me + (w - 2)) * S + c * LANES)).astype(F32)
-                    up = up + jnp.where(p == window, tail_rows[w][:, cut], 0.0)
-                    sk = kid_rows[w][0:1, cut]
-                    down = down + jnp.where(
-                        kid_rows[w][1:2, cut] == ids, sk * (head_rows[w][:, cut] - tail), 0.0
-                    )
-            parent_tail = jnp.sum(up, axis=1, keepdims=True)
-            inflow = jnp.sum(down, axis=1, keepdims=True)
-            head = jnp.where(has, s[:, 0:1] * (parent_tail - y[:, 0:1]), 0.0)
-            node = lax.broadcasted_iota(jnp.int32, (1, N), 1)
             step_up = jnp.where(node < N - 1, pltpu.roll(y, N - 1, 1) - y, 0.0)
-            edge = s * step_up
-            flux = edge - pltpu.roll(edge, 1, 1)
-            flux = flux + jnp.where(node == 0, head, 0.0) + jnp.where(node == N - 1, inflow, 0.0)
+            edge = sb[at, :] * step_up
+            flux = edge - pltpu.roll(edge, 1, 1) + ends[at, :]
             if old is None:
-                ptb[k, at, :] = jnp.broadcast_to(parent_tail, (step, LANES))
                 out[at, :] = y + time_step * (flux + ionic(y))
             else:
                 u = ys[old, at, :]
                 rise = jnp.where(node < N - 1, pltpu.roll(u, N - 1, 1) - u, 0.0)
-                inner = jnp.sum(-step_up * rise, axis=1, keepdims=True)
-                over = jnp.where(
-                    has, (y[:, 0:1] - parent_tail) * (ptb[old, at, 0:1] - u[:, 0:1]), 0.0
-                )
-                pgb[at, :] = pgb[at, :] + time_step * (inner + over)
+                pgb[at, :] = pgb[at, :] - time_step * (step_up * rise)
                 out[at, :] = y + time_step * (flux + slope(u) * y)
             return 0
 
@@ -496,7 +572,7 @@
             stores[-1].start()
             stores.append(pltpu.make_async_copy(mu0b, mu_o, loc_sem.at[9]))
             stores[-1].start()
-            gp_o[...] = jnp.transpose(pgb[...])[0:1, :]
+            gp_o[...] = pgr[...] + jnp.sum(jnp.transpose(pgb[...]), axis=0, keepdims=True)
 
             def finish(i, add):
                 l0b[i] = l0b[i] + add
@@ -535,27 +611,13 @@
     slots = D * cap
     rows = cx * cy
 
-    plane = cy * grid_y * cz
-    first = junction_voxel // plane
-    rest = junction_voxel % plane
-    second = rest // cz
-    third = rest % cz
-    owner = first // cx * grid_y + second // cy
-    local_voxel = (first % cx * cy + second % cy) * cz + third
-    local_node = junction_node % (S * N)
-    ordinal = jnp.arange(per_device, dtype=jnp.int32)
-    same = owner[:, None] == owner[None, :]
-    earlier = ordinal[:, None] < ordinal[None, :]
-    rank = jnp.sum((same & earlier).astype(jnp.int32), axis=0)
-    slot = owner * LANES + rank
-    match = jnp.arange(D * LANES, dtype=jnp.int32)[:, None] == slot[None, :]
-    slot_voxel = jnp.sum(jnp.where(match, local_voxel[None, :] + 1, 0), axis=1) - 1
-    slot_node = jnp.sum(jnp.where(match, local_node[None, :] + 1, 0), axis=1) - 1
-    slot_voxel = slot_voxel.astype(F32).reshape(D, 1, LANES)
-    slot_node = slot_node.astype(F32).reshape(D, 1, LANES)
+    chunks = S // LANES
+    window_rows = -(-3 * chunks // 16) * 16
+    kid_rows = -(-chunks // 16) * 16
 
     any_spec = pl.BlockSpec(memory_space=pl.ANY)
     vmem = pl.BlockSpec(memory_space=pltpu.VMEM)
+    hbm = pl.BlockSpec(memory_space=pltpu.HBM)
     V = pltpu.VMEM
     dma = pltpu.SemaphoreType.DMA
     field = V((cx, cy, cz), F32)
@@ -565,11 +627,12 @@
         V((cx, cy, cz), jnp.int32), V((cx, cy, cz), jnp.int32), V((cx + 1, cy, cz), F32),
         field, field, field, field, field, field, field,
         V((4, S, N), F32), fibre, fibre, V((S, N), jnp.int32), V((S, LANES), F32),
-        V((S, LANES), F32), V((2, S, LANES), F32), V((S, LANES), F32),
-        V((slots, rows), BF16), V((rows, slots), BF16), V((slots, cz), F32),
+        fibre, fibre, V((1, S), F32), V((2, 1, S), F32), V((LANES, S), BF16), V((window_rows, S), F32),
+        V((3 * S, LANES), BF16), V((kid_rows, 3 * S), F32), V((1, 3 * S), F32), V((kid_rows, LANES), F32),
+        V((slots, rows), BF16), V((rows, slots), BF16), V((slots, cz), F32), V((slots, cz), BF16),
         V((rows, 2 * cz), BF16), V((slots, 2 * cz), BF16),
-        V((slots, S), BF16), V((S, slots), BF16), V((slots, N), F32),
-        V((S, 2 * N), BF16), V((slots, 2 * N), BF16),
+        V((slots, S), BF16), V((S, slots), BF16), V((slots, N), F32), V((slots, N), BF16),
+        V((S, 2 * N), BF16), V((slots, 2 * N), BF16), V((D, 1, LANES), F32),
         V((LANES, LANES), F32), V((LANES, LANES), F32), V((LANES, LANES), F32),
         V((LANES, LANES), F32), V((slots, LANES), F32), V((slots, LANES), F32),
         V((4, D, 2, LANES), F32), V((4, D, 2, LANES), F32), V((D, 1, LANES), F32),
@@ -585,16 +648,16 @@
         functools.partial(kernel, grid_x, grid_y, cap),
         name="monodomain",
         out_shape=(tissue, cable, tissue, jax.ShapeDtypeStruct((1, S), F32), tissue, cable),
-        in_specs=[any_spec] * 5 + [vmem] * 2 + [any_spec] + [vmem] * 2,
+        in_specs=[hbm] * 5 + [vmem] * 2 + [hbm] + [vmem] * 2,
         out_specs=(any_spec, any_spec, any_spec, vmem, any_spec, any_spec),
         scratch_shapes=scratch,
         compiler_params=pltpu.CompilerParams(
-            collective_id=0, has_side_effects=True, vmem_limit_bytes=62 * 1024 * 1024
+            collective_id=0, has_side_effects=True, vmem_limit_bytes=36 * 1024 * 1024
         ),
     )(
         initial_voltage, conductivity, tissue_mask, target_step, initial_purkinje,
-        purkinje_conductivity.reshape(1, S), segment_parent.astype(F32).reshape(1, S),
-        purkinje_target, slot_voxel, slot_node,
+        purkinje_conductivity.reshape(1, S), segment_parent.reshape(1, S),
+        purkinje_target, junction_voxel.reshape(1, per_device), junction_node.reshape(1, per_device),
     )
     return v2, y2, gs, gp.reshape(S), la, mu
 

time: 73.7 us -> 72.1 us (0.978)
  local copies, waits for them, and re-layouts: 6.5 us -> 13.1 us
  other arithmetic: 4.66 us -> 0 us
  Pallas kernels: 61.6 us -> 58 us
    unnamed x16 -> x26, local copies, waits for them, and re-layouts: 6.5 us -> 13.1 us
    pallas_call x1, Pallas kernels: 61.6 us -> 58 us  [body(): pl.pallas_call(functools.partial(kernel, grid_x, grid_y, cap), name='mono...]
    convert_element_type x2 -> x0, other arithmetic: 1.87 us -> none  [the longest x1 1.26 us: body(): segment_parent.astype(F32).reshape(1, S)]
    add x3 -> x0, other arithmetic: 1.41 us -> none  [the longest x1 0.71 us: body(): local_voxel[None, :] + 1]
    reduce_sum x2 -> x0, other arithmetic: 1.38 us -> none  [the longest x1 1.21 us: body(): jnp.sum(jnp.where(match, local_node[None, :] + 1, 0), axis=1) - 1]
where the time goes in v1:
time: 72.1 us; the launch traced here: 71.7 us
  Pallas kernels  58 us (80%)
  local copies, waits for them, and re-layouts  13.1 us (18%)
    pallas_call x1, Pallas kernels, body(): pl.pallas_call(functools.partial(kernel, grid_x, grid_y, cap), name='mono...  58 us
    unnamed x26, local copies, waits for them, and re-layouts  13.1 us

profile of v1, /device:TPU:0, one launch (start us, length us, event | category | flops | bytes accessed | tf_op | source)
XLA Modules:
  0.0 71.7 jit_solution(1009583882260648488)
XLA Ops:
  0.6 0.0 copy-start.8
  0.6 0.0 copy-start.7
  0.7 0.0 copy-start.6
  0.7 0.7 copy-done.8
  1.3 0.0 copy-done.7
  1.3 0.0 copy-done.6
  1.4 0.0 copy-start
  1.4 1.2 %copy-done = f32[16,64,256]{2,1,0:T(8,128)S(1)} copy-done((f32[16,64,256]{2,1,0:T(8,128)S(1)}, f32[16,64,256]{2,1,0:T(8,128)}, u32[]{:S(2)}) %copy-start) | copy-done | bytes 1048600
  2.6 0.0 copy-start.1
  2.6 1.2 %copy-done.1 = f32[16,64,256]{2,1,0:T(8,128)S(1)} copy-done((f32[16,64,256]{2,1,0:T(8,128)S(1)}, f32[16,64,256]{2,1,0:T(8,128)}, u32[]{:S(2)}) %copy-start.1) | copy-done | bytes 1048600
  3.8 0.0 copy-start.2
  3.8 1.2 %copy-done.2 = s32[16,64,256]{2,1,0:T(8,128)S(1)} copy-done((s32[16,64,256]{2,1,0:T(8,128)S(1)}, s32[16,64,256]{2,1,0:T(8,128)}, u32[]{:S(2)}) %copy-start.2) | copy-done | bytes 1048600
  5.0 1.2 %copy-done.3 = s32[16,64,256]{2,1,0:T(8,128)S(1)} copy-done((s32[16,64,256]{2,1,0:T(8,128)S(1)}, s32[16,64,256]{2,1,0:T(8,128)}, u32[]{:S(2)}) %copy-start.3) | copy-done | bytes 1048600
  6.3 0.0 copy-start.4
  6.3 0.9 %copy-done.4 = f32[512,128]{1,0:T(8,128)S(1)} copy-done((f32[512,128]{1,0:T(8,128)S(1)}, f32[512,128]{1,0:T(8,128)}, u32[]{:S(2)}) %copy-start.4) | copy-done | bytes 262168
  7.2 0.9 %copy-done.5 = s32[512,128]{1,0:T(8,128)S(1)} copy-done((s32[512,128]{1,0:T(8,128)S(1)}, s32[512,128]{1,0:T(8,128)}, u32[]{:S(2)}) %copy-start.5) | copy-done | bytes 262168
  8.2 0.7 copy-done.9
  8.8 58.0 %monodomain.1 = (f32[16,64,256]{2,1,0:T(8,128)S(1)}, f32[512,128]{1,0:T(8,128)S(1)}, f32[16,64,256]{2,1,0:T(8,128)S(1)}, f32[1,512]{1,0:T(1,128)S(1)}, f32[16,64...) custom-call(f32[16,64,256]{2,1,0:T(8,128)S(1)} %copy-done, f32[16,64,256]{2,1,0:T(8,128)S(1)} %copy-done.1, ...), custom_call_target="tpu_custom_call" | custom-call | tf_op jit(solution)/shard_map/monodomain/pallas_call | solution.py:647
  66.8 1.0 %copy.22 = f32[16,64,256]{2,1,0:T(8,128)} copy(f32[16,64,256]{2,1,0:T(8,128)S(1)} %get-tuple-element.24) | data formatting | bytes 2097152
  67.8 0.7 copy.23
  68.5 1.0 %copy.24 = f32[16,64,256]{2,1,0:T(8,128)} copy(f32[16,64,256]{2,1,0:T(8,128)S(1)} %get-tuple-element.26) | data formatting | bytes 2097152
  69.5 0.6 copy.25
  70.0 1.0 %copy.26 = f32[16,64,256]{2,1,0:T(8,128)} copy(f32[16,64,256]{2,1,0:T(8,128)S(1)} %get-tuple-element.28) | data formatting | bytes 2097152
  71.0 0.7 copy.27
  (3 shorter events, 0.0 us)
Async XLA Ops:
  0.6 0.7 copy-start.8
  0.6 0.7 copy-start.7
  0.7 0.7 copy-start.6
  1.4 1.2 %copy-start = (f32[16,64,256]{2,1,0:T(8,128)S(1)}, f32[16,64,256]{2,1,0:T(8,128)}, u32[]{:S(2)}) copy-start(f32[16,64,256]{2,1,0:T(8,128)} %v0_h.1) | copy-start | bytes 3145732
  2.6 1.2 %copy-start.1 = (f32[16,64,256]{2,1,0:T(8,128)S(1)}, f32[16,64,256]{2,1,0:T(8,128)}, u32[]{:S(2)}) copy-start(f32[16,64,256]{2,1,0:T(8,128)} %sigma_h.1) | copy-start | bytes 3145732
  3.8 1.2 %copy-start.2 = (s32[16,64,256]{2,1,0:T(8,128)S(1)}, s32[16,64,256]{2,1,0:T(8,128)}, u32[]{:S(2)}) copy-start(s32[16,64,256]{2,1,0:T(8,128)} %mask_h.1) | copy-start | bytes 3145732
  5.0 1.2 %copy-start.3 = (s32[16,64,256]{2,1,0:T(8,128)S(1)}, s32[16,64,256]{2,1,0:T(8,128)}, u32[]{:S(2)}) copy-start(s32[16,64,256]{2,1,0:T(8,128)} %target_h.1) | copy-start | bytes 3145732
  6.3 0.9 %copy-start.4 = (f32[512,128]{1,0:T(8,128)S(1)}, f32[512,128]{1,0:T(8,128)}, u32[]{:S(2)}) copy-start(f32[512,128]{1,0:T(8,128)} %y0_h.1) | copy-start | bytes 786436
  7.2 0.9 %copy-start.5 = (s32[512,128]{1,0:T(8,128)S(1)}, s32[512,128]{1,0:T(8,128)}, u32[]{:S(2)}) copy-start(s32[512,128]{1,0:T(8,128)} %ptarget_h.1) | copy-start | bytes 786436
  8.2 0.7 copy-start.9

commit v2 on v1

--- a/solution.py
+++ b/solution.py
@@ -181,7 +181,7 @@
     def side_copy(k):
         return rc(hys.at[k], hyr.at[k], ysm_s.at[k], ysm_r.at[k], {"gx": gx, "gy": 1 - gy})
 
-    def halo_start(k):
+    def planes_start(k):
         @pl.when(gx < grid_x - 1)
         def _():
             up_copy(k).start()
@@ -190,6 +190,8 @@
         def _():
             down_copy(k).start()
 
+    def halo_start(k):
+        planes_start(k)
         side_copy(k).start()
 
     def halo_wait(k):
@@ -438,7 +440,7 @@
         else:
             over = (own_heads - parent_tail) * (ptr[old] - heads[old])
             pgr[...] = pgr[...] + time_step * jnp.where(has_parent, over, 0.0)
-        step = 64
+        step = min(S, 256)
         node = lax.broadcasted_iota(jnp.int32, (1, N), 1)
 
         def part(b, _):
@@ -460,16 +462,30 @@
 
     group = 4 if cx % 4 == 0 else 1
 
-    def spread(finish):
-        def step(b, _):
+    def spread(finish, between=None):
+        def step(b):
             at = pl.ds(pl.multiple_of(b * (group * cy), group * cy), group * cy)
             add = dot(ott[at, :], ws[...])
             add = add[:, :cz] + add[:, cz:]
             for g in range(group):
                 finish(b * group + g, add[g * cy : (g + 1) * cy])
+
+        groups = cx // group
+
+        def outer(b, _):
+            step(b * (groups - 1))
             return 0
 
-        lax.fori_loop(0, cx // group, step, 0)
+        def inner(b, _):
+            step(b)
+            return 0
+
+        lax.fori_loop(0, 2, outer, 0)
+        if between is not None:
+            planes_start(between)
+        lax.fori_loop(1, groups - 1, inner, 0)
+        if between is not None:
+            side_copy(between).start()
 
     def spread_cable():
         add = dot(opt[...], wps[...])
@@ -520,8 +536,7 @@
                 hys[2, pl.ds(i, 1), :] = edge_row(seed)
                 split_plane(i, seed)
         cable_start(k + 1)
-        spread(finish)
-        halo_start(k + 1)
+        spread(finish, k + 1)
 
     stores = [
         pltpu.make_async_copy(v2b, v2_o, loc_sem.at[6]),
@@ -576,9 +591,7 @@
 
             def finish(i, add):
                 l0b[i] = l0b[i] + add
-        spread(finish)
-        if k == 2:
-            halo_start(3)
+        spread(finish, 3 if k == 2 else None)
 
     stores.append(pltpu.make_async_copy(l0b, la_o, loc_sem.at[10]))
     stores[-1].start()
@@ -592,6 +605,15 @@
         for c in cable_copies(k):
             c.wait_send()
     for c in stores:
+        c.wait()
+
+
+def put_out(*refs):
+    n = (len(refs) - 1) // 2
+    copies = [pltpu.make_async_copy(refs[i], refs[n + i], refs[-1].at[i]) for i in range(n)]
+    for c in copies:
+        c.start()
+    for c in copies:
         c.wait()
 
 
@@ -655,10 +677,21 @@
             collective_id=0, has_side_effects=True, vmem_limit_bytes=36 * 1024 * 1024
         ),
     )(
-        initial_voltage, conductivity, tissue_mask, target_step, initial_purkinje,
+        *[pltpu.with_memory_space_constraint(a, pltpu.HBM) for a in (
+            initial_voltage, conductivity, tissue_mask, target_step, initial_purkinje)],
         purkinje_conductivity.reshape(1, S), segment_parent.reshape(1, S),
-        purkinje_target, junction_voxel.reshape(1, per_device), junction_node.reshape(1, per_device),
+        pltpu.with_memory_space_constraint(purkinje_target, pltpu.HBM), junction_voxel.reshape(1, per_device), junction_node.reshape(1, per_device),
     )
+    results = (v2, y2, gs, gp, la, mu)
+    v2, y2, gs, gp, la, mu = pl.pallas_call(
+        put_out,
+        name="put_out",
+        out_shape=tuple(jax.ShapeDtypeStruct(r.shape, r.dtype) for r in results),
+        in_specs=[any_spec] * 6,
+        out_specs=(hbm,) * 6,
+        scratch_shapes=[dma((6,))],
+        compiler_params=pltpu.CompilerParams(vmem_limit_bytes=1024 * 1024),
+    )(*results)
     return v2, y2, gs, gp.reshape(S), la, mu
 
 

time: 72.1 us -> 55.5 us (0.77)
  local copies, waits for them, and re-layouts: 13.1 us -> 1.37 us
  Pallas kernels: 58 us -> 53.2 us
    unnamed x26 -> x8, local copies, waits for them, and re-layouts: 13.1 us -> 1.37 us
    pallas_call x1, Pallas kernels: 58 us -> 51.3 us  [body(): pl.pallas_call(functools.partial(kernel, grid_x, grid_y, cap), name='mono...]
    pallas_call x0 -> x1, Pallas kernels: none -> 1.88 us  [body(): pl.pallas_call(put_out, name='put_out', out_shape=tuple((jax.ShapeDtypeSt...]
where the time goes in v2:
time: 55.5 us; the launch traced here: 55.3 us
  Pallas kernels  53.2 us (96%)
  local copies, waits for them, and re-layouts  1.37 us (2%)
  between operations  0.67 us (1%)
    pallas_call x1, Pallas kernels, body(): pl.pallas_call(functools.partial(kernel, grid_x, grid_y, cap), name='mono...  51.3 us
    pallas_call x1, Pallas kernels, body(): pl.pallas_call(put_out, name='put_out', out_shape=tuple((jax.ShapeDtypeSt...  1.88 us
    unnamed x8, local copies, waits for them, and re-layouts  1.37 us

profile of v2, /device:TPU:0, one launch (start us, length us, event | category | flops | bytes accessed | tf_op | source)
XLA Modules:
  0.0 55.3 jit_solution(7421122370240471578)
XLA Ops:
  0.6 0.0 copy-start.2
  0.6 0.0 copy-start.1
  0.7 0.0 copy-start
  0.7 0.7 %copy-done.2 = s32[512]{0:T(512)S(1)} copy-done((s32[512]{0:T(512)S(1)}, s32[512]{0:T(512)}, u32[]{:S(2)}) %copy-start.2) | copy-done | bytes 2072
  1.3 0.0 copy-done.1
  1.3 0.0 copy-done
  1.4 0.0 copy-start.3
  1.4 0.7 %copy-done.3 = s32[512]{0:T(512)S(1)} copy-done((s32[512]{0:T(512)S(1)}, s32[512]{0:T(512)}, u32[]{:S(2)}) %copy-start.3) | copy-done | bytes 2072
  2.0 51.3 %monodomain.1 = (f32[16,64,256]{2,1,0:T(8,128)S(1)}, f32[512,128]{1,0:T(8,128)S(1)}, f32[16,64,256]{2,1,0:T(8,128)S(1)}, f32[1,512]{1,0:T(1,128)S(1)}, f32[16,64...) custom-call(f32[16,64,256]{2,1,0:T(8,128)} %v0_h.1, f32[16,64,256]{2,1,0:T(8,128)} %sigma_h.1, s32[16,64,256]{2,1,0:T(8,128)} %mask_h.1, ...), custom_call_target="tpu_custom_call" | custom-call | tf_op jit(solution)/shard_map/monodomain/pallas_call | solution.py:669
  53.4 1.9 %put_out.1 = (f32[16,64,256]{2,1,0:T(8,128)}, f32[512,128]{1,0:T(8,128)}, f32[16,64,256]{2,1,0:T(8,128)}, f32[1,512]{1,0:T(1,128)}, f32[16,64,256]{2,1,0:T(8,128)}, /*index=5*/f32[512,128]{1,0:T(8,128)}) custom-call(f32[16,64,256]{2,1,0:T(8,128)S(1)} %get-tuple-element.18.refs_0_, f32[512,128]{1,0:T(8,128)S(1)} %get-tuple-element.19.refs_1_, ...), custom_call_target="tpu_custom_call" | custom-call | tf_op jit(solution)/shard_map/put_out/pallas_call | solution.py:686
Async XLA Ops:
  0.6 0.7 %copy-start.2 = (s32[512]{0:T(512)S(1)}, s32[512]{0:T(512)}, u32[]{:S(2)}) copy-start(s32[512]{0:T(512)} %param.18) | copy-start | bytes 6148
  0.6 0.7 %copy-start.1 = (s32[512]{0:T(512)S(1)}, s32[512]{0:T(512)}, u32[]{:S(2)}) copy-start(s32[512]{0:T(512)} %param.16) | copy-start | bytes 6148
  0.7 0.7 %copy-start = (f32[512]{0:T(512)S(1)}, f32[512]{0:T(512)}, u32[]{:S(2)}) copy-start(f32[512]{0:T(512)} %param.15) | copy-start | bytes 6148
  1.4 0.7 %copy-start.3 = (s32[512]{0:T(512)S(1)}, s32[512]{0:T(512)}, u32[]{:S(2)}) copy-start(s32[512]{0:T(512)} %param.19) | copy-start | bytes 6148
